TPU v7x, 128 devices: a whole 4x4x4 slice. The times are simulated.
128 devices in a mesh: dp: 4 (over y), expert: 4 (over x), tensor: 8 (over z, core).
Axes of the slice: x: 4, y: 4, z: 4, core: 2. Of those that a mesh axis runs over, the one named last changes fastest.
Arguments:
- tokens: bfloat16 [2048, 6144], P(('dp', 'expert'), 'tensor'), may hold values from -6 to 6
- grad_out: bfloat16 [2048, 6144], P(('dp', 'expert'), 'tensor'), may hold values from -6 to 6
- expert_ids: int32 [2048, 4], P(('dp', 'expert')), may hold values from 0 to 15, all different within a row; in each aligned block of 128 rows (0 to 127, 128 to 255, ...) at most 48 rows name the same one
- gate_fixed: int32 [2048, 4], P(('dp', 'expert')), may hold values from 8192 to 65535
- w_gate: bfloat16 [4, 5376, 6144], P('expert', ('dp', 'tensor')), may hold values from -0.078125 to 0.078125
- w_up: bfloat16 [4, 5376, 6144], P('expert', ('dp', 'tensor')), may hold values from -0.078125 to 0.078125
- w_down: bfloat16 [4, 5376, 6144], P('expert', ('dp', 'tensor')), may hold values from -0.078125 to 0.078125
Outputs:
- mixed: bfloat16 [2048, 6144], P(('dp', 'expert'), 'tensor')
- grad_tokens: bfloat16 [2048, 6144], P(('dp', 'expert'), 'tensor')
- grad_gate: float32 [4, 5376, 6144], P('expert', ('dp', 'tensor'))
- grad_up: float32 [4, 5376, 6144], P('expert', ('dp', 'tensor'))
- grad_down: float32 [4, 5376, 6144], P('expert', ('dp', 'tensor'))
Inputs may be any that keep to these rules, and one draw needn't show every extreme that they name: `expert_ids`: each row names 4 different experts; in each aligned block of 128 rows no expert is named by more than 48 rows, a bound that some block reaches.
All inputs are finite; a program needn't handle non-finite values.
Results may differ from a plain program's by a relative error of at most 0.02.
Values may be sent and summed in bfloat16 or wider, within the bound.
No kernel may reach another device: no remote copies, remote signals or barrier semaphores. Data moves between devices by JAX's collectives and lax.ppermute only.
A program may use at most 128 MiB of HBM per device.

v0:
```python
import jax
import jax.numpy as jnp
from jax import lax
from jax.sharding import PartitionSpec as P

CAP = 48


def in_one_piece(arrays, axis, dim, along):
    ends, at = ([], 0)
    for a in arrays[:-1]:
        at += a.shape[along]
        ends.append(at)
    both = jnp.concatenate(arrays, axis=along)
    return tuple(jnp.split(lax.all_gather(both, axis, axis=dim, tiled=True), ends, axis=along))


def in_one_piece_2(arrays, axis, split_dim, concat_dim, along):
    widths = [a.shape[along] for a in arrays]
    both = jnp.concatenate(arrays, axis=along)
    whole = lax.all_to_all(both, axis, split_axis=split_dim, concat_axis=concat_dim, tiled=True)
    return tuple(jnp.split(whole, [sum(widths[:k]) for k in range(1, len(widths))], axis=along))


def joined_along(parts, dim):
    parts = jnp.moveaxis(parts, 0, dim)
    lengths = parts.shape
    return parts.reshape(*lengths[:dim], lengths[dim] * lengths[dim + 1], *lengths[dim + 2 :])


def copy_for_each(shard, axis):
    copies = jnp.broadcast_to(shard, (lax.axis_size(axis), *shard.shape))
    return lax.all_to_all(copies, axis, split_axis=0, concat_axis=0, tiled=True)


def gather_directly(shard, axis, dim):
    return joined_along(copy_for_each(shard, axis), dim)


def in_one_piece_3(arrays, axis, dim, along):
    ends, at = ([], 0)
    for a in arrays[:-1]:
        at += a.shape[along]
        ends.append(at)
    both = jnp.concatenate(arrays, axis=along)
    return tuple(jnp.split(gather_directly(both, axis, dim), ends, axis=along))


def slot_tables(expert_ids, gate_fixed, expert_count):
    gate_value = gate_fixed.astype(jnp.float32) * (1.0 / 65536.0)
    matches = expert_ids[:, :, None] == jnp.arange(expert_count, dtype=jnp.int32)[None, None, :]
    chosen = jnp.any(matches, axis=1).astype(jnp.int32)
    weight = jnp.sum(jnp.where(matches, gate_value[:, :, None], 0.0), axis=1)
    slot_rank = jnp.cumsum(chosen, axis=0) - chosen
    in_slot = (slot_rank[:, :, None] == jnp.arange(CAP, dtype=jnp.int32)[None, None, :]) & (
        chosen[:, :, None] > 0
    )
    slot_table = jnp.transpose(in_slot.astype(jnp.float32), (1, 2, 0))
    slot_gate = jnp.einsum("jct,tj->jc", slot_table, weight, precision=lax.Precision.HIGHEST)
    return (slot_table, slot_gate)


def full_features(first_part, second_part):
    return in_one_piece((first_part, second_part), "tensor", 1, 0)


def on_device(tokens, grad_out, expert_ids, gate_fixed, w_gate, w_up, w_down):
    expert_count = lax.axis_size("expert")
    tensor_count = lax.axis_size("tensor")
    feat_width = tokens.shape[1]
    slot_table, slot_gate = slot_tables(expert_ids, gate_fixed, expert_count)
    table_half = slot_table.astype(jnp.bfloat16)
    send_rows = jnp.einsum(
        "jct,tf->jcf", table_half, tokens, preferred_element_type=jnp.float32
    ).astype(jnp.bfloat16)
    send_cots = jnp.einsum("jct,tf->jcf", table_half, grad_out, preferred_element_type=jnp.float32)
    send_cots = (send_cots * slot_gate[:, :, None]).astype(jnp.bfloat16)
    got_rows, got_cots = in_one_piece_2((send_rows, send_cots), "expert", 0, 0, 1)
    block_rows = expert_count * CAP
    got_rows = got_rows.reshape(block_rows, feat_width)
    got_cots = got_cots.reshape(block_rows, feat_width)
    panel_gate = w_gate[0]
    panel_up = w_up[0]
    panel_down = w_down[0]
    slab_rows, slab_cots = in_one_piece_3((got_rows, got_cots), "dp", 0, 1)
    all_rows, all_cots = full_features(slab_rows, slab_cots)
    gate_pre = lax.dot_general(
        all_rows, panel_gate, (((1,), (1,)), ((), ())), preferred_element_type=jnp.float32
    )
    up_pre = lax.dot_general(
        all_rows, panel_up, (((1,), (1,)), ((), ())), preferred_element_type=jnp.float32
    )
    gate_sig = jax.nn.sigmoid(gate_pre)
    hid_piece = (gate_pre * gate_sig * up_pre).astype(jnp.bfloat16)
    hid_grad = lax.dot_general(
        all_cots, panel_down, (((1,), (1,)), ((), ())), preferred_element_type=jnp.float32
    )
    dg_piece = (hid_grad * up_pre * gate_sig * (1.0 + gate_pre * (1.0 - gate_sig))).astype(
        jnp.bfloat16
    )
    du_piece = (hid_grad * gate_pre * gate_sig).astype(jnp.bfloat16)
    grad_g = lax.dot_general(
        dg_piece, all_rows, (((0,), (0,)), ((), ())), preferred_element_type=jnp.float32
    )
    grad_u = lax.dot_general(
        du_piece, all_rows, (((0,), (0,)), ((), ())), preferred_element_type=jnp.float32
    )
    grad_d = lax.dot_general(
        hid_piece, all_cots, (((0,), (0,)), ((), ())), preferred_element_type=jnp.float32
    )
    state = (hid_piece, dg_piece, du_piece, grad_g, grad_u, grad_d)
    hidden, d_gate, d_up, grad_g, grad_u, grad_d = state

    def one_block(block_index):
        dp_block = block_index // tensor_count
        tensor_block = block_index % tensor_count
        hid_rows = lax.dynamic_slice_in_dim(hidden, dp_block * block_rows, block_rows, 0)
        dg_rows = lax.dynamic_slice_in_dim(d_gate, dp_block * block_rows, block_rows, 0)
        du_rows = lax.dynamic_slice_in_dim(d_up, dp_block * block_rows, block_rows, 0)
        down_cols = lax.dynamic_slice_in_dim(panel_down, tensor_block * feat_width, feat_width, 1)
        gate_cols = lax.dynamic_slice_in_dim(panel_gate, tensor_block * feat_width, feat_width, 1)
        up_cols = lax.dynamic_slice_in_dim(panel_up, tensor_block * feat_width, feat_width, 1)
        out_block = jnp.dot(hid_rows, down_cols, preferred_element_type=jnp.float32)
        back_block = jnp.dot(dg_rows, gate_cols, preferred_element_type=jnp.float32)
        back_block = back_block + jnp.dot(du_rows, up_cols, preferred_element_type=jnp.float32)
        return jnp.concatenate([out_block, back_block], axis=1)

    block_terms = lax.map(
        one_block,
        jnp.arange(block_rows * lax.axis_size(("dp", "tensor")) // block_rows, dtype=jnp.int32),
    )
    summed = lax.psum_scatter(
        block_terms.reshape(block_rows * lax.axis_size(("dp", "tensor")), 2 * feat_width).astype(
            jnp.bfloat16
        ),
        ("dp", "tensor"),
        scatter_dimension=0,
        tiled=True,
    ).astype(jnp.float32)
    summed = summed.astype(jnp.bfloat16).reshape(expert_count, CAP, 2 * feat_width)
    returned = lax.all_to_all(summed, "expert", split_axis=0, concat_axis=0, tiled=True)
    expert_out = returned[:, :, :feat_width].astype(jnp.float32) * slot_gate[:, :, None]
    expert_back = returned[:, :, feat_width:].astype(jnp.float32)
    mixed = jnp.einsum(
        "jct,jcf->tf", slot_table, expert_out, precision=lax.Precision.HIGHEST
    ).astype(jnp.bfloat16)
    grad_tokens = jnp.einsum(
        "jct,jcf->tf", slot_table, expert_back, precision=lax.Precision.HIGHEST
    ).astype(jnp.bfloat16)
    return (mixed, grad_tokens, grad_g[None], grad_u[None], grad_d[None])


def solution(mesh):
    return jax.shard_map(
        on_device,
        mesh=mesh,
        in_specs=(
            P(("dp", "expert"), "tensor"),
            P(("dp", "expert"), "tensor"),
            P(("dp", "expert"), None),
            P(("dp", "expert"), None),
            P("expert", ("dp", "tensor"), None),
            P("expert", ("dp", "tensor"), None),
            P("expert", ("dp", "tensor"), None),
        ),
        out_specs=(
            P(("dp", "expert"), "tensor"),
            P(("dp", "expert"), "tensor"),
            P("expert", ("dp", "tensor"), None),
            P("expert", ("dp", "tensor"), None),
            P("expert", ("dp", "tensor"), None),
        ),
        check_vma=False,
    )
```

profile of v0, /device:TPU:0, one launch (start us, length us, event | category | flops | bytes accessed | tf_op | source)
XLA Modules:
  0.0 541.2 jit_solution(3950452015644500439)
XLA Ops:
  11.4 14.4 %all_to_all.15 = bf16[4,96,768]{2,1,0:T(8,128)(2,1)S(1)} all-to-all(bf16[4,96,768]{2,1,0:T(8,128)(2,1)S(1)} %pad_maximum_fusion.1), channel_id=1, replica_groups=mesh['dp'=4,'expert'=4,'tensor'=8] {'expert'}, dimensions={0} | all-to-all | bytes 1179648 | tf_op jit(solution)/shard_map/all_to_all | solution.py:21
  26.0 32.0 %all_to_all.16 = bf16[4,192,1536]{2,1,0:T(8,128)(2,1)S(1)} all-to-all(bf16[4,192,1536]{2,1,0:T(8,128)(2,1)S(1)} %broadcast_in_dim.45), channel_id=1, replica_groups=mesh['dp'=4,'expert'=4,'tensor'=8] {'dp'}, dimensions={0} | all-to-all | bytes 4718592 | tf_op jit(solution)/shard_map/all_to_all | solution.py:33
  58.2 1.6 pad_maximum_fusion
  59.8 92.5 %all-gather.2.cloned.1.call-done = bf16[1536,6144]{1,0:T(8,128)(2,1)} async-done(((bf16[1536,768]{1,0:T(8,128)(2,1)}), bf16[1536,6144]{1,0:T(8,128)(2,1)}) %all-gather.2.cloned.1.call-update) | async-done | bytes 18874384 | tf_op jit(solution)/shard_map/all_gather | solution.py:15
  152.3 7.7 %fusion.21 = f32[768,168]{0,1:T(8,128)S(1)} fusion(bf16[1536,6144]{1,0:T(8,128)(2,1)} %all-gather.2.cloned.1.call-done, bf16[1,168,6144]{2,1,0:T(8,128)(2,1)} %param.14), kind=kOutput, calls=%fused_computation.23 | convolution fusion | flops 1585446912 | bytes 12017664 | tf_op jit(solution)/shard_map/dot_general | solution.py:90
  160.0 7.8 %fusion.23 = f32[768,168]{0,1:T(8,128)S(1)} fusion(bf16[1536,6144]{1,0:T(8,128)(2,1)} %all-gather.2.cloned.1.call-done, bf16[1,168,6144]{2,1,0:T(8,128)(2,1)S(1)} %copy-done.2), kind=kOutput, calls=%fused_computation.25 | convolution fusion | flops 1585446912 | bytes 12017664 | tf_op jit(solution)/shard_map/dot_general | solution.py:87
  167.9 3.4 multiply_convert_fusion
  171.3 225.3 %while.12 = (s32[]{:T(128)}, bf16[32,192,1536]{2,1,0:T(8,128)(2,1)}, s32[32]{0:T(128)S(1)}, bf16[768,168]{0,1:T(8,128)(2,1)S(1)}, bf16[168,6144]{1,0:T(8,128)(2,...) while((s32[]{:T(128)}, ...), condition=%wide.region_4.5_spmd, body=%wide.region_3.4_spmd.sunk | while | flops 150110240 | bytes 3982304 | solution.py:128
  174.9 1.3 convolution_add_fusion.2
  176.2 1.3 fusion.76
  181.9 1.3 convolution_add_fusion.2
  183.2 1.3 fusion.76
  188.9 1.3 convolution_add_fusion.2
  190.3 1.3 fusion.76
  196.0 1.3 convolution_add_fusion.2
  197.3 1.3 fusion.76
  203.0 1.3 convolution_add_fusion.2
  204.3 1.3 fusion.76
  210.0 1.3 convolution_add_fusion.2
  211.3 1.3 fusion.76
  217.1 1.3 convolution_add_fusion.2
  218.4 1.3 fusion.76
  224.1 1.3 convolution_add_fusion.2
  225.4 1.3 fusion.76
  231.2 1.3 convolution_add_fusion.2
  232.5 1.3 fusion.76
  238.2 1.3 convolution_add_fusion.2
  239.5 1.3 fusion.76
  245.2 1.3 convolution_add_fusion.2
  246.5 1.3 fusion.76
  252.3 1.3 convolution_add_fusion.2
  253.6 1.3 fusion.76
  259.4 1.3 convolution_add_fusion.2
  260.7 1.3 fusion.76
  266.4 1.3 convolution_add_fusion.2
  267.7 1.3 fusion.76
  273.4 1.3 convolution_add_fusion.2
  274.8 1.3 fusion.76
  280.5 1.3 convolution_add_fusion.2
  281.8 1.3 fusion.76
  287.6 1.3 convolution_add_fusion.2
  294.6 1.3 convolution_add_fusion.2
  301.6 1.3 convolution_add_fusion.2
  308.7 1.3 convolution_add_fusion.2
  310.0 1.3 fusion.76
  315.7 1.3 convolution_add_fusion.2
  322.7 1.3 convolution_add_fusion.2
  324.0 1.3 fusion.76
  329.8 1.3 convolution_add_fusion.2
  336.9 1.3 convolution_add_fusion.2
  343.9 1.3 convolution_add_fusion.2
  350.9 1.3 convolution_add_fusion.2
  358.0 1.3 convolution_add_fusion.2
  365.0 1.3 convolution_add_fusion.2
  372.1 1.3 convolution_add_fusion.2
  373.4 1.3 fusion.76
  379.1 1.3 convolution_add_fusion.2
  386.1 1.3 convolution_add_fusion.2
  393.2 1.3 convolution_add_fusion.2
  396.7 7.5 %convolution_bitcast_fusion = f32[1,168,6144]{2,1,0:T(8,128)} fusion(bf16[768,168]{0,1:T(8,128)(2,1)S(1)} %get-tuple-element.294, bf16[1536,6144]{1,0:T(8,128)(2,1)} %all-gather.2.cloned.1.call-done), kind=kOutput, calls=%fused_computation.19 | convolution fusion | flops 1585446912 | bytes 13824000 | tf_op jit(solution)/shard_map/dot_general | solution.py:105
  404.1 8.2 %fusion.16 = f32[1,168,6144]{2,1,0:T(8,128)} fusion(bf16[768,168]{0,1:T(8,128)(2,1)S(1)} %get-tuple-element.292, bf16[1536,6144]{1,0:T(8,128)(2,1)} %all-gather.2.cloned.1.call-done), kind=kOutput, calls=%fused_computation.18 | convolution fusion | flops 1585446912 | bytes 13824000 | tf_op jit(solution)/shard_map/dot_general | solution.py:108
  412.3 106.9 %reduce-scatter.2.cloned.1.call-done = bf16[192,1536]{1,0:T(8,128)(2,1)} async-done(((bf16[6144,1536]{1,0:T(8,128)(2,1)}), bf16[192,1536]{1,0:T(8,128)(2,1)}) %reduce-scatter.2.cloned.1.call-update) | async-done | bytes 589840 | tf_op jit(solution)/shard_map/reduce_scatter | solution.py:132
  519.2 4.3 all-to-all-start.2
  523.5 7.5 %convolution_bitcast_fusion.1 = f32[1,168,6144]{2,1,0:T(8,128)} fusion(bf16[768,168]{0,1:T(8,128)(2,1)S(1)} %get-tuple-element.293, bf16[1536,6144]{1,0:T(8,128)(2,1)} %all-gather.2.cloned.1.call-done), kind=kOutput, calls=%fused_computation.20 | convolution fusion | flops 1585446912 | bytes 13824000 | tf_op jit(solution)/shard_map/dot_general | solution.py:102
  (144 shorter events, 82.4 us)
Async XLA Ops:
  7.2 2.7 copy-start
  7.2 145.1 %all-gather.2.cloned.1.call-start = ((), (), s32[]{:S(2)}) async-start(), calls=%async_computation.4 | async-start | bytes 21233664 | tf_op jit(solution)/shard_map/all_gather | solution.py:15
  59.7 459.5 %reduce-scatter.2.cloned.1.call-start = ((), (), s32[]{:S(2)}) async-start(), calls=%async_computation.5 | async-start | bytes 19464192 | tf_op jit(solution)/shard_map/reduce_scatter | solution.py:132
  59.8 100.2 %copy-start.2 = (bf16[1,168,6144]{2,1,0:T(8,128)(2,1)S(1)}, bf16[1,168,6144]{2,1,0:T(8,128)(2,1)}, u32[]{:S(2)}) copy-start(bf16[1,168,6144]{2,1,0:T(8,128)(2,1)} %param.13) | copy-start | bytes 6193156
  152.3 15.5 %copy-start.4 = (bf16[1536,6144]{1,0:T(8,128)(2,1)S(1)}, bf16[1536,6144]{1,0:T(8,128)(2,1)}, u32[]{:S(2)}) copy-start(bf16[1536,6144]{1,0:T(8,128)(2,1)} %all-gather.2.cloned.1.call-done) | copy-start | bytes 56623108
  160.0 7.8 %copy-start.3 = (bf16[1,168,6144]{2,1,0:T(8,128)(2,1)S(1)}, bf16[1,168,6144]{2,1,0:T(8,128)(2,1)}, u32[]{:S(2)}) copy-start(bf16[1,168,6144]{2,1,0:T(8,128)(2,1)} %param.15) | copy-start | bytes 6193156
  519.2 13.0 %all-to-all-start.2 = ((bf16[4,48,1536]{2,1,0:T(8,128)(2,1)}), bf16[4,48,1536]{2,1,0:T(8,128)(2,1)S(1)}, u32[]{:S(2)}, u32[]{:S(2)}) async-start(bf16[4,48,1536]{2,1,0:T(8,128)(2,1)} %bitcast.65), calls=%async_computation.3 | async-start | bytes 1179648 | tf_op jit(solution)/shard_map/all_to_all | solution.py:141
  523.5 10.8 %copy-start.1 = (bf16[128,768]{1,0:T(8,128)(2,1)S(1)}, bf16[128,768]{1,0:T(8,128)(2,1)}, u32[]{:S(2)}) copy-start(bf16[128,768]{1,0:T(8,128)(2,1)} %param.9) | copy-start | bytes 589828
Sparse Core Ops, SparseCore 0:
  59.9 92.4 all-gather.1
  396.8 122.3 reduce-scatter.1
where the time goes:
time: 545 us; the launch traced here: 541 us
  waiting for transfers between devices  201 us (37%)
  matrix products  140 us (26%)
  loops' own time  84.6 us (16%)
  blocking collectives  46.4 us (9%)
  other arithmetic  32 us (6%)
  local copies, waits for them, and re-layouts  19.2 us (4%)
  between operations  14.2 us (3%)
    reduce_scatter x1, waiting for transfers between devices, on_device(): lax.psum_scatter(block_terms.reshape(block_rows * lax.axis_size(('dp', 't...  107 us
    all_gather x1, waiting for transfers between devices, in_one_piece(): lax.all_gather(both, axis, axis=dim, tiled=True)  92.5 us
    another operation x1, loops' own time, on_device(): lax.map(one_block, jnp.arange(block_rows * lax.axis_size(('dp', 'tensor')...  84.6 us
    dot_general x32, matrix products, one_block(): jnp.dot(du_rows, up_cols, preferred_element_type=jnp.float32)  41.6 us
    dot_general x32, matrix products, one_block(): out_block = jnp.dot(hid_rows, down_cols, preferred_element_type=jnp.float32)  41.5 us
    all_to_all x1, blocking collectives, copy_for_each(): return lax.all_to_all(copies, axis, split_axis=0, concat_axis=0, tiled=True)  32 us
    dynamic_update_slice x32, other arithmetic, on_device(): lax.map(one_block, jnp.arange(block_rows * lax.axis_size(('dp', 'tensor')...  28 us
    dynamic_slice x32, local copies, waits for them, and re-layouts, on_device(): lax.map(one_block, jnp.arange(block_rows * lax.axis_size(('dp', 'tensor')...  18.6 us
  transfers between devices with their start and end apart: 3, of which 3 were waited for; matrix products, arithmetic and copies ran while one was open for 4% of the time, Pallas kernels for 0%

commit v1 on v0

v1 whole, which is shorter than its diff:
```python
import jax
import jax.numpy as jnp
from jax import lax
from jax.experimental import pallas as pl
from jax.experimental.pallas import tpu as pltpu
from jax.sharding import Mesh
from jax.sharding import PartitionSpec as P

CAP = 48
VMEM_LIMIT = 48 * 1024 * 1024
PLANE = ("dp", "z")
SWAP = [(0, 1), (1, 0)]


def slot_tables(expert_ids, gate_fixed, expert_count):
    gate_value = gate_fixed.astype(jnp.float32) * (1.0 / 65536.0)
    matches = expert_ids[:, :, None] == jnp.arange(expert_count, dtype=jnp.int32)[None, None, :]
    chosen = jnp.any(matches, axis=1).astype(jnp.int32)
    weight = jnp.sum(jnp.where(matches, gate_value[:, :, None], 0.0), axis=1)
    slot_rank = jnp.cumsum(chosen, axis=0) - chosen
    in_slot = (slot_rank[:, :, None] == jnp.arange(CAP, dtype=jnp.int32)[None, None, :]) & (
        chosen[:, :, None] > 0
    )
    slot_table = jnp.transpose(in_slot.astype(jnp.float32), (1, 2, 0))
    slot_gate = jnp.einsum("jct,tj->jc", slot_table, weight, precision=lax.Precision.HIGHEST)
    return (slot_table, slot_gate)


def dot(a, b, dims):
    return lax.dot_general(a, b, (dims, ((), ())), preferred_element_type=jnp.float32)


def params(semantics=("arbitrary",)):
    return pltpu.CompilerParams(dimension_semantics=semantics, vmem_limit_bytes=VMEM_LIMIT)


def pack_columns(core, w_gate, w_up, w_down, z_count, width):
    hidden = w_gate.shape[1]

    def kernel(core_ref, g_ref, u_ref, d_ref, out_ref):
        out_ref[0, 0] = g_ref[0]
        out_ref[1, 0] = u_ref[0]
        out_ref[2, 0] = d_ref[0]

    spec = pl.BlockSpec((1, hidden, width), lambda z, core_ref: (0, 0, 2 * z + 1 - core_ref[0]))
    return pl.pallas_call(
        kernel,
        out_shape=jax.ShapeDtypeStruct((3, z_count, hidden, width), w_gate.dtype),
        grid_spec=pltpu.PrefetchScalarGridSpec(
            num_scalar_prefetch=1,
            grid=(z_count,),
            in_specs=[spec, spec, spec],
            out_specs=pl.BlockSpec((3, 1, hidden, width), lambda z, core_ref: (0, z, 0, 0)),
        ),
        compiler_params=params(),
        cost_estimate=pl.CostEstimate(
            flops=0, bytes_accessed=12 * z_count * hidden * width, transcendentals=0
        ),
        name="pack_columns",
    )(core, w_gate, w_up, w_down)


def forward(gathered, w_gate, w_up, w_down):
    dp, tensor, _, slots, width = gathered.shape
    rows = dp * slots
    hidden = w_gate.shape[1]

    def kernel(x_ref, g_ref, u_ref, d_ref, out_ref, gate_acc, up_acc, dhid_acc):
        t = pl.program_id(0)
        toks = x_ref[:, 0, 0].reshape(rows, width)
        cots = x_ref[:, 0, 1].reshape(rows, width)
        last = ((1,), (1,))
        gate_part = dot(g_ref[0], toks, last)
        up_part = dot(u_ref[0], toks, last)
        dhid_part = dot(d_ref[0], cots, last)

        @pl.when(t == 0)
        def _():
            gate_acc[...] = gate_part
            up_acc[...] = up_part
            dhid_acc[...] = dhid_part

        @pl.when(t > 0)
        def _():
            gate_acc[...] += gate_part
            up_acc[...] += up_part
            dhid_acc[...] += dhid_part

        @pl.when(t == tensor - 1)
        def _():
            gate = gate_acc[...]
            up = up_acc[...]
            dhid = dhid_acc[...]
            sig = jax.nn.sigmoid(gate)
            out_ref[0] = (gate * sig * up).astype(out_ref.dtype)
            out_ref[1] = (dhid * up * sig * (1.0 + gate * (1.0 - sig))).astype(out_ref.dtype)
            out_ref[2] = (dhid * gate * sig).astype(out_ref.dtype)

    w_spec = pl.BlockSpec((1, hidden, width), lambda t: (0, 0, t))
    return pl.pallas_call(
        kernel,
        out_shape=jax.ShapeDtypeStruct((3, hidden, rows), gathered.dtype),
        grid=(tensor,),
        in_specs=[
            pl.BlockSpec((dp, 1, 2, slots, width), lambda t: (0, t, 0, 0, 0)),
            w_spec,
            w_spec,
            w_spec,
        ],
        out_specs=pl.BlockSpec((3, hidden, rows), lambda t: (0, 0, 0)),
        scratch_shapes=[pltpu.VMEM((hidden, rows), jnp.float32)] * 3,
        compiler_params=params(),
        cost_estimate=pl.CostEstimate(
            flops=6 * rows * hidden * width * tensor,
            bytes_accessed=(4 * rows + 6 * hidden) * width * tensor,
            transcendentals=rows * hidden,
        ),
        name="forward",
    )(gathered, w_gate, w_up, w_down)


def block_products(core, mine, other, w_gate, w_up, w_down, other_cols, dp):
    _, hidden, rows = mine.shape
    _, z_count, _, width = other_cols.shape
    slots = rows // dp

    def kernel(core_ref, mt_ref, ot_ref, g_ref, u_ref, d_ref, oc_ref, out_ref, m_ref, o_ref):
        inner = ((1,), (0,))

        @pl.when(pl.program_id(0) == 0)
        def _():
            for k in range(3):
                m_ref[k] = mt_ref[k].T
                o_ref[k] = ot_ref[k].T

        out = dot(m_ref[0], d_ref[0], inner) + dot(o_ref[0], oc_ref[2, 0], inner)
        out_ref[:, 0, :, :width] = out.astype(out_ref.dtype).reshape(dp, slots, width)
        back = dot(m_ref[1], g_ref[0], inner) + dot(o_ref[1], oc_ref[0, 0], inner)
        back = back + dot(m_ref[2], u_ref[0], inner) + dot(o_ref[2], oc_ref[1, 0], inner)
        out_ref[:, 0, :, width:] = back.astype(out_ref.dtype).reshape(dp, slots, width)

    acts = pl.BlockSpec((3, hidden, rows), lambda z, core_ref: (0, 0, 0))
    cols = pl.BlockSpec((1, hidden, width), lambda z, core_ref: (0, 0, 2 * z + core_ref[0]))
    return pl.pallas_call(
        kernel,
        out_shape=jax.ShapeDtypeStruct((dp, z_count, slots, 2 * width), mine.dtype),
        grid_spec=pltpu.PrefetchScalarGridSpec(
            num_scalar_prefetch=1,
            grid=(z_count,),
            in_specs=[
                acts,
                acts,
                cols,
                cols,
                cols,
                pl.BlockSpec((3, 1, hidden, width), lambda z, core_ref: (0, z, 0, 0)),
            ],
            out_specs=pl.BlockSpec(
                (dp, 1, slots, 2 * width), lambda z, core_ref: (0, z, 0, 0)
            ),
            scratch_shapes=[pltpu.VMEM((3, rows, hidden), mine.dtype)] * 2,
        ),
        compiler_params=params(),
        cost_estimate=pl.CostEstimate(
            flops=12 * rows * hidden * width * z_count,
            bytes_accessed=(4 * rows + 12 * hidden) * width * z_count,
            transcendentals=0,
        ),
        name="block_products",
    )(core, mine, other, w_gate, w_up, w_down, other_cols)


def weight_grads(acts_t, gathered):
    dp, tensor, _, slots, width = gathered.shape
    _, hidden, rows = acts_t.shape

    def kernel(a_ref, x_ref, g_ref, u_ref, d_ref):
        toks = x_ref[:, 0, 0].reshape(rows, width)
        cots = x_ref[:, 0, 1].reshape(rows, width)
        inner = ((1,), (0,))
        g_ref[0] = dot(a_ref[1], toks, inner)
        u_ref[0] = dot(a_ref[2], toks, inner)
        d_ref[0] = dot(a_ref[0], cots, inner)

    out = jax.ShapeDtypeStruct((1, hidden, tensor * width), jnp.float32)
    o_spec = pl.BlockSpec((1, hidden, width), lambda t: (0, 0, t))
    return pl.pallas_call(
        kernel,
        out_shape=(out, out, out),
        grid=(tensor,),
        in_specs=[
            pl.BlockSpec((3, hidden, rows), lambda t: (0, 0, 0)),
            pl.BlockSpec((dp, 1, 2, slots, width), lambda t: (0, t, 0, 0, 0)),
        ],
        out_specs=(o_spec, o_spec, o_spec),
        compiler_params=params(),
        cost_estimate=pl.CostEstimate(
            flops=6 * rows * hidden * width * tensor,
            bytes_accessed=(4 * rows + 12 * hidden) * width * tensor,
            transcendentals=0,
        ),
        name="weight_grads",
    )(acts_t, gathered)


def on_device(tokens, grad_out, expert_ids, gate_fixed, w_gate, w_up, w_down):
    expert_count = lax.axis_size("expert")
    dp_count = lax.axis_size("dp")
    z_count = lax.axis_size("z")
    width = tokens.shape[1]
    core = lax.axis_index("core").astype(jnp.int32).reshape(1)
    slot_table, slot_gate = slot_tables(expert_ids, gate_fixed, expert_count)
    table_half = slot_table.astype(jnp.bfloat16)
    send_rows = jnp.einsum(
        "jct,tf->jcf", table_half, tokens, preferred_element_type=jnp.float32
    ).astype(jnp.bfloat16)
    send_cots = jnp.einsum("jct,tf->jcf", table_half, grad_out, preferred_element_type=jnp.float32)
    send_cots = (send_cots * slot_gate[:, :, None]).astype(jnp.bfloat16)
    got = lax.all_to_all(
        jnp.concatenate([send_rows, send_cots], axis=1),
        "expert",
        split_axis=0,
        concat_axis=0,
        tiled=True,
    )
    slots = expert_count * CAP
    shard = jnp.concatenate(
        [got[:, :CAP].reshape(slots, width), got[:, CAP:].reshape(slots, width)], axis=0
    )
    core, shard = lax.optimization_barrier((core, shard))
    gathered = lax.all_gather(shard, ("dp", "z", "core"), axis=0, tiled=True)
    gathered = gathered.reshape(dp_count, z_count * 2, 2, slots, width)
    packed = pack_columns(core, w_gate, w_up, w_down, z_count, width)
    other_cols = lax.ppermute(packed, "core", SWAP)
    mine = forward(gathered, w_gate, w_up, w_down)
    other = lax.ppermute(mine, "core", SWAP)
    terms = block_products(core, mine, other, w_gate, w_up, w_down, other_cols, dp_count)
    summed = lax.psum_scatter(
        terms.reshape(dp_count * z_count * slots, 2 * width),
        PLANE,
        scatter_dimension=0,
        tiled=True,
    )
    grad_g, grad_u, grad_d = weight_grads(mine, gathered)
    summed, grad_g, grad_u, grad_d = lax.optimization_barrier((summed, grad_g, grad_u, grad_d))
    summed = summed.reshape(expert_count, CAP, 2 * width)
    returned = lax.all_to_all(summed, "expert", split_axis=0, concat_axis=0, tiled=True)
    expert_out = returned[:, :, :width].astype(jnp.float32) * slot_gate[:, :, None]
    expert_back = returned[:, :, width:].astype(jnp.float32)
    mixed = jnp.einsum(
        "jct,jcf->tf", slot_table, expert_out, precision=lax.Precision.HIGHEST
    ).astype(jnp.bfloat16)
    grad_tokens = jnp.einsum(
        "jct,jcf->tf", slot_table, expert_back, precision=lax.Precision.HIGHEST
    ).astype(jnp.bfloat16)
    return (mixed, grad_tokens, grad_g, grad_u, grad_d)


def solution(mesh):
    dp, expert, tensor = (mesh.shape[a] for a in ("dp", "expert", "tensor"))
    fine = Mesh(mesh.devices.reshape(dp, expert, tensor // 2, 2), ("dp", "expert", "z", "core"))
    feats = P(("dp", "expert"), ("z", "core"))
    ids = P(("dp", "expert"), None)
    weights = P("expert", ("dp", "z", "core"), None)
    return jax.shard_map(
        on_device,
        mesh=fine,
        in_specs=(feats, feats, ids, ids, weights, weights, weights),
        out_specs=(feats, feats, weights, weights, weights),
        check_vma=False,
    )
```

time: 545 us -> 247 us (0.45)
  matrix products: 140 us -> 3.69 us
  loops' own time: 84.6 us -> 0 us
  Pallas kernels: 0 us -> 43.2 us
  waiting for transfers between devices: 201 us -> 158 us
  blocking collectives: 46.4 us -> 13.1 us
  other arithmetic: 32 us -> 4.01 us
  local copies, waits for them, and re-layouts: 19.2 us -> 4.96 us
    dot_general x102 -> x0, matrix products: 136 us -> none  [the longest x32 41.6 us: one_block(): jnp.dot(du_rows, up_cols, preferred_element_type=jnp.float32)]
    another operation x1 -> x0, loops' own time: 84.6 us -> none  [on_device(): lax.map(one_block, jnp.arange(block_rows * lax.axis_size(('dp', 'tensor')...]
    pallas_call x0 -> x4, Pallas kernels: none -> 43.2 us  [the longest x1 14.6 us: weight_grads(): pl.pallas_call(kernel, out_shape=(out, out, out), grid=(tensor,), in_spec...]
    reduce_scatter x1, waiting for transfers between devices: 107 us -> 73 us  [on_device(): lax.psum_scatter(terms.reshape(dp_count * z_count * slots, 2 * width), PL...]
    all_to_all x2 -> x1, blocking collectives: 46.4 us -> 13.1 us  [on_device(): lax.all_to_all(summed, 'expert', split_axis=0, concat_axis=0, tiled=True)]
    dynamic_update_slice x32 -> x0, other arithmetic: 28 us -> none  [on_device(): lax.map(one_block, jnp.arange(block_rows * lax.axis_size(('dp', 'tensor')...]
    all_gather x1, waiting for transfers between devices: 92.5 us -> 72.6 us  [on_device(): gathered = lax.all_gather(shard, ('dp', 'z', 'core'), axis=0, tiled=True)]
    dynamic_slice x32 -> x0, local copies, waits for them, and re-layouts: 18.6 us -> none  [on_device(): lax.map(one_block, jnp.arange(block_rows * lax.axis_size(('dp', 'tensor')...]
  transfers between devices with their start and end apart: 3 -> 5, of which waited for: 3 -> 4; matrix products, arithmetic and copies ran while one was open for 4% -> 0% of each run, Pallas kernels for 0% -> 13%
where the time goes in v1:
time: 247 us; the launch traced here: 246 us
  waiting for transfers between devices  158 us (64%)
  Pallas kernels  43.2 us (17%)
  between operations  14.1 us (6%)
  blocking collectives  13.1 us (5%)
  local copies, waits for them, and re-layouts  4.96 us (2%)
  starting transfers between devices  4.91 us (2%)
  other arithmetic  4.01 us (2%)
  matrix products  3.69 us (1%)
    reduce_scatter x1, waiting for transfers between devices, on_device(): lax.psum_scatter(terms.reshape(dp_count * z_count * slots, 2 * width), PL...  73 us
    all_gather x1, waiting for transfers between devices, on_device(): gathered = lax.all_gather(shard, ('dp', 'z', 'core'), axis=0, tiled=True)  72.6 us
    pallas_call x1, Pallas kernels, weight_grads(): pl.pallas_call(kernel, out_shape=(out, out, out), grid=(tensor,), in_spec...  14.6 us
    pallas_call x1, Pallas kernels, forward(): pl.pallas_call(kernel, out_shape=jax.ShapeDtypeStruct((3, hidden, rows),...  14.5 us
    all_to_all x1, blocking collectives, on_device(): lax.all_to_all(summed, 'expert', split_axis=0, concat_axis=0, tiled=True)  13.1 us
    pallas_call x1, Pallas kernels, block_products(): pl.pallas_call(kernel, out_shape=jax.ShapeDtypeStruct((dp, z_count, slots...  11.7 us
    all_to_all x1, waiting for transfers between devices, on_device(): lax.all_to_all(jnp.concatenate([send_rows, send_cots], axis=1), 'expert',...  10.2 us
  transfers between devices with their start and end apart: 5, of which 4 were waited for; matrix products, arithmetic and copies ran while one was open for 0% of the time, Pallas kernels for 13%

profile of v1, /device:TPU:0, one launch (start us, length us, event | category | flops | bytes accessed | tf_op | source)
XLA Modules:
  0.0 245.8 jit_solution(12357162732810834879)
XLA Ops:
  7.2 0.0 copy-start
  7.2 0.7 fusion.25
  7.9 0.7 convert_multiply_fusion
  8.6 0.7 select_reduce_fusion
  9.3 0.1 copy.22
  9.4 0.2 reduce_window_sum.11
  9.6 0.1 copy.23
  9.7 0.2 fusion.13
  9.9 0.0 copy-done
  9.9 0.2 convolution_convert_fusion
  10.1 1.1 fusion
  11.3 0.9 pad_maximum_fusion
  12.1 0.0 copy-start.1
  12.1 4.5 %all-to-all-start = ((bf16[4,96,768]{2,1,0:T(8,128)(2,1)}), bf16[4,96,768]{2,1,0:T(8,128)(2,1)S(1)}, u32[]{:S(2)}, u32[]{:S(2)}) async-start(bf16[4,96,768]{2,1,0:T(8,128)(2,1)} %pad_maximum_fusion), calls=%async_computation | async-start | bytes 1179648 | tf_op jit(solution)/shard_map/all_to_all | solution.py:219
  16.7 0.0 all-gather.2.cloned.1.call-start
  16.7 10.2 %all-to-all-done = bf16[4,96,768]{2,1,0:T(8,128)(2,1)S(1)} async-done(((bf16[4,96,768]{2,1,0:T(8,128)(2,1)}), bf16[4,96,768]{2,1,0:T(8,128)(2,1)S(1)}, u32[]{:S(2)}, u32[]{:S(2)}) %all-to-all-start) | async-done | bytes 589856 | tf_op jit(solution)/shard_map/all_to_all | solution.py:219
  26.9 0.9 pad_maximum_fusion.1
  27.7 0.0 all-gather.2.cloned.1.call-update
  27.8 0.0 reduce-scatter.2.cloned.1.call-start
  27.8 0.0 copy-done.1
  27.8 0.0 copy-start.2
  27.8 1.6 copy-done.2
  29.4 0.0 copy-start.4
  29.4 1.6 copy-done.4
  31.0 2.3 pack_columns.1
  33.3 0.0 collective-permute-start.1
  33.3 72.6 %all-gather.2.cloned.1.call-done = bf16[12288,768]{1,0:T(8,128)(2,1)} async-done(((bf16[384,768]{1,0:T(8,128)(2,1)}), bf16[12288,768]{1,0:T(8,128)(2,1)}) %all-gather.2.cloned.1.call-update) | async-done | bytes 18874384 | tf_op jit(solution)/shard_map/all_gather | solution.py:231
  106.0 0.0 copy-start.3
  106.0 1.6 copy-done.3
  107.5 14.5 %forward.1.mt_ref.a_ref = bf16[3,168,768]{2,1,0:T(8,128)(2,1)S(1)} custom-call(bf16[4,8,2,192,768]{4,3,2,1,0:T(8,128)(2,1)} %bitcast.30, bf16[1,168,6144]{2,1,0:T(8,128)(2,1)S(1)} %copy-done.1, bf16[1,168,6144]{2,1,0:T(8,128)(2,1)S(1)} %copy-done.3, bf16[1,168,6144]{2,1,0:T(8,128)(2,1)} %d_ref.5), custom_call_target="tpu_custom_call" | custom-call | flops 4756340736 | bytes 25067520 | tf_op jit(solution)/shard_map/forward/pallas_call | solution.py:100
  122.1 0.3 collective-permute-start
  122.4 0.0 collective-permute-done.1.oc_ref
  122.4 2.0 collective-permute-done.ot_ref
  124.4 11.7 %block_products.1 = bf16[4,4,192,1536]{3,2,1,0:T(8,128)(2,1)} custom-call(s32[1]{0:T(128)} %bitcast.2.core_ref, bf16[3,168,768]{2,1,0:T(8,128)(2,1)S(1)} %forward.1.mt_ref.a_ref, bf16[3,168,768]{2,1,0:T(8,128)(2,1)S(1)} %collective-permute-done.ot_ref, bf16[1,168,6144]{2,1,0:T(8,128)(2,1)S(1)} %copy-done.1, bf16[1,168,6144]{2,1,0:T(8,128)(2,1)S(1)} %copy-done.3, ...), custom_call_target="tpu_custom_call" | custom-call | flops 4756340736 | bytes 15630336 | tf_op jit(solution)/shard_map/block_products/pallas_call | solution.py:144
  136.2 0.0 reduce-scatter.2.cloned.1.call-update
  136.2 14.6 %weight_grads.1 = (f32[1,168,6144]{2,1,0:T(8,128)}, f32[1,168,6144]{2,1,0:T(8,128)}, f32[1,168,6144]{2,1,0:T(8,128)}) custom-call(bf16[3,168,768]{2,1,0:T(8,128)(2,1)S(1)} %forward.1.mt_ref.a_ref, bf16[4,8,2,192,768]{4,3,2,1,0:T(8,128)(2,1)} %bitcast.31), custom_call_target="tpu_custom_call" | custom-call | flops 4756340736 | bytes 31260672 | tf_op jit(solution)/shard_map/weight_grads/pallas_call | solution.py:187
  150.8 73.0 %reduce-scatter.2.cloned.1.call-done = bf16[192,1536]{1,0:T(8,128)(2,1)} async-done(((bf16[3072,1536]{1,0:T(8,128)(2,1)}), bf16[192,1536]{1,0:T(8,128)(2,1)}) %reduce-scatter.2.cloned.1.call-update) | async-done | bytes 589840 | tf_op jit(solution)/shard_map/reduce_scatter | solution.py:238
  223.8 13.1 %all_to_all.10 = bf16[4,48,1536]{2,1,0:T(8,128)(2,1)S(1)} all-to-all(bf16[4,48,1536]{2,1,0:T(8,128)(2,1)} %bitcast.35), channel_id=1, replica_groups=mesh['dp'=4,'expert'=4,'z'=4,'core'=2] {'expert'}, dimensions={0} | all-to-all | bytes 1179648 | tf_op jit(solution)/shard_map/all_to_all | solution.py:247
  236.9 1.2 fusion.1
  238.1 0.9 fusion.2
  (3 shorter events, 0.1 us)
Async XLA Ops:
  7.2 2.7 %copy-start = (bf16[128,768]{1,0:T(8,128)(2,1)S(1)}, bf16[128,768]{1,0:T(8,128)(2,1)}, u32[]{:S(2)}) copy-start(bf16[128,768]{1,0:T(8,128)(2,1)} %param.7) | copy-start | bytes 589828
  12.1 15.7 %copy-start.1 = (bf16[1,168,6144]{2,1,0:T(8,128)(2,1)S(1)}, bf16[1,168,6144]{2,1,0:T(8,128)(2,1)}, u32[]{:S(2)}) copy-start(bf16[1,168,6144]{2,1,0:T(8,128)(2,1)} %g_ref.5) | copy-start | bytes 6193156
  12.1 14.7 %all-to-all-start = ((bf16[4,96,768]{2,1,0:T(8,128)(2,1)}), bf16[4,96,768]{2,1,0:T(8,128)(2,1)S(1)}, u32[]{:S(2)}, u32[]{:S(2)}) async-start(bf16[4,96,768]{2,1,0:T(8,128)(2,1)} %pad_maximum_fusion), calls=%async_computation | async-start | bytes 1179648 | tf_op jit(solution)/shard_map/all_to_all | solution.py:219
  16.7 89.3 %all-gather.2.cloned.1.call-start = ((), (), s32[]{:S(2)}) async-start(), calls=%async_computation.3 | async-start | bytes 19464192 | tf_op jit(solution)/shard_map/all_gather | solution.py:231
  27.8 196.0 %reduce-scatter.2.cloned.1.call-start = ((), (), s32[]{:S(2)}) async-start(), calls=%async_computation.4 | async-start | bytes 10027008 | tf_op jit(solution)/shard_map/reduce_scatter | solution.py:238
  27.8 1.6 copy-start.2
  29.4 1.6 copy-start.4
  33.3 89.1 %collective-permute-start.1 = (bf16[3,4,168,768]{3,2,1,0:T(8,128)(2,1)}, bf16[3,4,168,768]{3,2,1,0:T(8,128)(2,1)}, u32[]{:S(2)}, u32[]{:S(2)}) collective-permute-start(bf16[3,4,168,768]{3,2,1,0:T(8,128)(2,1)} %pack_columns.1), channel_id=1, source_target_pairs={{0,1},{1,0},{2,3},{3,2},{4,5},{5,4},{6,7},{7,6},{8,9},{9,8},{10,11... | collective-permute-start | bytes 9289736 | tf_op jit(solution)/shard_map/ppermute | solution.py:234
  106.0 1.6 copy-start.3
  122.1 2.3 collective-permute-start
Sparse Core Ops, SparseCore 0:
  27.9 78.0 all-gather.1
  136.3 87.4 reduce-scatter.1

commit v2 on v1

v2 whole, which is shorter than its diff:
```python
import jax
import jax.numpy as jnp
from jax import lax
from jax.experimental import pallas as pl
from jax.experimental.pallas import tpu as pltpu
from jax.sharding import Mesh
from jax.sharding import PartitionSpec as P

CAP = 48
VMEM_LIMIT = 48 * 1024 * 1024
PLANE = ("dp", "z")
SWAP = [(0, 1), (1, 0)]


def slot_tables(expert_ids, gate_fixed, expert_count):
    gate_value = gate_fixed.astype(jnp.float32) * (1.0 / 65536.0)
    matches = expert_ids[:, :, None] == jnp.arange(expert_count, dtype=jnp.int32)[None, None, :]
    chosen = jnp.any(matches, axis=1).astype(jnp.int32)
    weight = jnp.sum(jnp.where(matches, gate_value[:, :, None], 0.0), axis=1)
    slot_rank = jnp.cumsum(chosen, axis=0) - chosen
    in_slot = (slot_rank[:, :, None] == jnp.arange(CAP, dtype=jnp.int32)[None, None, :]) & (
        chosen[:, :, None] > 0
    )
    slot_table = jnp.transpose(in_slot.astype(jnp.float32), (1, 2, 0))
    slot_gate = jnp.einsum("jct,tj->jc", slot_table, weight, precision=lax.Precision.HIGHEST)
    return (slot_table, slot_gate)


def dot(a, b, dims):
    return lax.dot_general(a, b, (dims, ((), ())), preferred_element_type=jnp.float32)


def params(semantics=("arbitrary",)):
    return pltpu.CompilerParams(dimension_semantics=semantics, vmem_limit_bytes=VMEM_LIMIT)


def pack_columns(core, w_gate, w_up, w_down, z_count, width):
    hidden = w_gate.shape[1]

    def kernel(core_ref, g_ref, u_ref, d_ref, out_ref):
        out_ref[0, 0] = g_ref[0]
        out_ref[1, 0] = u_ref[0]
        out_ref[2, 0] = d_ref[0]

    spec = pl.BlockSpec((1, hidden, width), lambda z, core_ref: (0, 0, 2 * z + 1 - core_ref[0]))
    return pl.pallas_call(
        kernel,
        out_shape=jax.ShapeDtypeStruct((3, z_count, hidden, width), w_gate.dtype),
        grid_spec=pltpu.PrefetchScalarGridSpec(
            num_scalar_prefetch=1,
            grid=(z_count,),
            in_specs=[spec, spec, spec],
            out_specs=pl.BlockSpec((3, 1, hidden, width), lambda z, core_ref: (0, z, 0, 0)),
        ),
        compiler_params=params(),
        cost_estimate=pl.CostEstimate(
            flops=0, bytes_accessed=12 * z_count * hidden * width, transcendentals=0
        ),
        name="pack_columns",
    )(core, w_gate, w_up, w_down)


def forward(core, gathered, w_gate, w_up, w_down, other_cols):
    dp, z_count, _, slots, width = gathered.shape
    rows = dp * slots
    hidden = w_gate.shape[1]

    def kernel(core_ref, x_ref, g_ref, u_ref, d_ref, oc_ref, sum_ref, send_ref):
        z = pl.program_id(0)
        toks = x_ref[:, 0, 0].reshape(rows, width)
        cots = x_ref[:, 0, 1].reshape(rows, width)
        weights = (g_ref[0], u_ref[0], d_ref[0], oc_ref[0, 0], oc_ref[1, 0], oc_ref[2, 0])
        for k, w in enumerate(weights):
            part = dot(w, cots if k % 3 == 2 else toks, ((1,), (1,)))

            @pl.when(z == 0)
            def _(k=k, part=part):
                sum_ref[k] = part

            @pl.when(z > 0)
            def _(k=k, part=part):
                sum_ref[k] += part

        @pl.when(z == z_count - 1)
        def _():
            for k in range(6):
                send_ref[k] = sum_ref[k].astype(send_ref.dtype)

    cols = pl.BlockSpec((1, hidden, width), lambda z, core_ref: (0, 0, 2 * z + core_ref[0]))
    whole = pl.BlockSpec((6, hidden, rows), lambda z, core_ref: (0, 0, 0))
    return pl.pallas_call(
        kernel,
        out_shape=[
            jax.ShapeDtypeStruct((6, hidden, rows), jnp.float32),
            jax.ShapeDtypeStruct((6, hidden, rows), gathered.dtype),
        ],
        grid_spec=pltpu.PrefetchScalarGridSpec(
            num_scalar_prefetch=1,
            grid=(z_count,),
            in_specs=[
                pl.BlockSpec((dp, 1, 2, slots, width), lambda z, core_ref: (0, z, 0, 0, 0)),
                cols,
                cols,
                cols,
                pl.BlockSpec((3, 1, hidden, width), lambda z, core_ref: (0, z, 0, 0)),
            ],
            out_specs=[whole, whole],
        ),
        compiler_params=params(),
        cost_estimate=pl.CostEstimate(
            flops=12 * rows * hidden * width * z_count,
            bytes_accessed=(4 * rows + 12 * hidden) * width * z_count,
            transcendentals=0,
        ),
        name="forward",
    )(core, gathered, w_gate, w_up, w_down, other_cols)


def block_products(core, sums, got, w_gate, w_up, w_down, other_cols, dp):
    _, hidden, rows = sums.shape
    _, z_count, _, width = other_cols.shape
    slots = rows // dp
    half = other_cols.dtype

    def kernel(core_ref, s_ref, r_ref, g_ref, u_ref, d_ref, oc_ref, out_ref, act_ref, m_ref, o_ref):
        inner = ((1,), (0,))

        @pl.when(pl.program_id(0) == 0)
        def _():
            for at, turned in ((0, m_ref), (3, o_ref)):
                there = 3 - at
                gate = s_ref[at] + r_ref[there].astype(jnp.float32)
                up = s_ref[at + 1] + r_ref[there + 1].astype(jnp.float32)
                dhid = s_ref[at + 2] + r_ref[there + 2].astype(jnp.float32)
                sig = jax.nn.sigmoid(gate)
                acts = (
                    gate * sig * up,
                    dhid * up * sig * (1.0 + gate * (1.0 - sig)),
                    dhid * gate * sig,
                )
                for k, act in enumerate(acts):
                    act = act.astype(half)
                    act_ref[at + k] = act
                    turned[k] = act.T

        out = dot(m_ref[0], d_ref[0], inner) + dot(o_ref[0], oc_ref[2, 0], inner)
        out_ref[:, 0, :, :width] = out.astype(half).reshape(dp, slots, width)
        back = dot(m_ref[1], g_ref[0], inner) + dot(o_ref[1], oc_ref[0, 0], inner)
        back = back + dot(m_ref[2], u_ref[0], inner) + dot(o_ref[2], oc_ref[1, 0], inner)
        out_ref[:, 0, :, width:] = back.astype(half).reshape(dp, slots, width)

    whole = pl.BlockSpec((6, hidden, rows), lambda z, core_ref: (0, 0, 0))
    cols = pl.BlockSpec((1, hidden, width), lambda z, core_ref: (0, 0, 2 * z + core_ref[0]))
    return pl.pallas_call(
        kernel,
        out_shape=[
            jax.ShapeDtypeStruct((dp, z_count, slots, 2 * width), half),
            jax.ShapeDtypeStruct((6, hidden, rows), half),
        ],
        grid_spec=pltpu.PrefetchScalarGridSpec(
            num_scalar_prefetch=1,
            grid=(z_count,),
            in_specs=[
                whole,
                whole,
                cols,
                cols,
                cols,
                pl.BlockSpec((3, 1, hidden, width), lambda z, core_ref: (0, z, 0, 0)),
            ],
            out_specs=[
                pl.BlockSpec((dp, 1, slots, 2 * width), lambda z, core_ref: (0, z, 0, 0)),
                whole,
            ],
            scratch_shapes=[pltpu.VMEM((3, rows, hidden), half)] * 2,
        ),
        compiler_params=params(),
        cost_estimate=pl.CostEstimate(
            flops=12 * rows * hidden * width * z_count,
            bytes_accessed=(4 * rows + 12 * hidden) * width * z_count,
            transcendentals=2 * rows * hidden,
        ),
        name="block_products",
    )(core, sums, got, w_gate, w_up, w_down, other_cols)


def weight_grads(core, acts, gathered):
    dp, z_count, _, slots, width = gathered.shape
    _, hidden, rows = acts.shape

    def kernel(core_ref, a_ref, x_ref, g_ref, u_ref, d_ref, away_ref):
        toks = x_ref[:, 0, 0].reshape(rows, width)
        cots = x_ref[:, 0, 1].reshape(rows, width)
        inner = ((1,), (0,))
        g_ref[0] = dot(a_ref[1], toks, inner)
        u_ref[0] = dot(a_ref[2], toks, inner)
        d_ref[0] = dot(a_ref[0], cots, inner)
        away_ref[0, 0] = dot(a_ref[4], toks, inner)
        away_ref[1, 0] = dot(a_ref[5], toks, inner)
        away_ref[2, 0] = dot(a_ref[3], cots, inner)

    out = jax.ShapeDtypeStruct((1, hidden, 2 * z_count * width), jnp.float32)
    cols = pl.BlockSpec((1, hidden, width), lambda z, core_ref: (0, 0, 2 * z + core_ref[0]))
    return pl.pallas_call(
        kernel,
        out_shape=[out] * 3 + [jax.ShapeDtypeStruct((3, z_count, hidden, width), jnp.float32)],
        grid_spec=pltpu.PrefetchScalarGridSpec(
            num_scalar_prefetch=1,
            grid=(z_count,),
            in_specs=[
                pl.BlockSpec((6, hidden, rows), lambda z, core_ref: (0, 0, 0)),
                pl.BlockSpec((dp, 1, 2, slots, width), lambda z, core_ref: (0, z, 0, 0, 0)),
            ],
            out_specs=[cols] * 3
            + [pl.BlockSpec((3, 1, hidden, width), lambda z, core_ref: (0, z, 0, 0))],
        ),
        compiler_params=params(),
        cost_estimate=pl.CostEstimate(
            flops=12 * rows * hidden * width * z_count,
            bytes_accessed=(4 * rows + 24 * hidden) * width * z_count,
            transcendentals=0,
        ),
        name="weight_grads",
    )(core, acts, gathered)


def fill_columns(core, grads, got):
    _, z_count, hidden, width = got.shape

    def kernel(core_ref, got_ref, g_in, u_in, d_in, g_ref, u_ref, d_ref):
        g_ref[0] = got_ref[0, 0]
        u_ref[0] = got_ref[1, 0]
        d_ref[0] = got_ref[2, 0]

    cols = pl.BlockSpec((1, hidden, width), lambda z, core_ref: (0, 0, 2 * z + 1 - core_ref[0]))
    return pl.pallas_call(
        kernel,
        out_shape=[jax.ShapeDtypeStruct(g.shape, g.dtype) for g in grads],
        grid_spec=pltpu.PrefetchScalarGridSpec(
            num_scalar_prefetch=1,
            grid=(z_count,),
            in_specs=[pl.BlockSpec((3, 1, hidden, width), lambda z, core_ref: (0, z, 0, 0))]
            + [pl.BlockSpec(memory_space=pl.ANY)] * 3,
            out_specs=[cols] * 3,
        ),
        input_output_aliases={2: 0, 3: 1, 4: 2},
        compiler_params=params(),
        cost_estimate=pl.CostEstimate(
            flops=0, bytes_accessed=24 * z_count * hidden * width, transcendentals=0
        ),
        name="fill_columns",
    )(core, got, *grads)


def on_device(tokens, grad_out, expert_ids, gate_fixed, w_gate, w_up, w_down):
    expert_count = lax.axis_size("expert")
    dp_count = lax.axis_size("dp")
    z_count = lax.axis_size("z")
    width = tokens.shape[1]
    core = lax.axis_index("core").astype(jnp.int32).reshape(1)
    slot_table, slot_gate = slot_tables(expert_ids, gate_fixed, expert_count)
    table_half = slot_table.astype(jnp.bfloat16)
    send_rows = jnp.einsum(
        "jct,tf->jcf", table_half, tokens, preferred_element_type=jnp.float32
    ).astype(jnp.bfloat16)
    send_cots = jnp.einsum("jct,tf->jcf", table_half, grad_out, preferred_element_type=jnp.float32)
    send_cots = (send_cots * slot_gate[:, :, None]).astype(jnp.bfloat16)
    got = lax.all_to_all(
        jnp.concatenate([send_rows, send_cots], axis=1),
        "expert",
        split_axis=0,
        concat_axis=0,
        tiled=True,
    )
    slots = expert_count * CAP
    shard = jnp.concatenate(
        [got[:, :CAP].reshape(slots, width), got[:, CAP:].reshape(slots, width)], axis=0
    )
    core, shard = lax.optimization_barrier((core, shard))
    gathered = lax.all_gather(shard, PLANE, axis=0, tiled=True)
    gathered = gathered.reshape(dp_count, z_count, 2, slots, width)
    packed = pack_columns(core, w_gate, w_up, w_down, z_count, width)
    other_cols = lax.ppermute(packed, "core", SWAP)
    sums, sent = forward(core, gathered, w_gate, w_up, w_down, other_cols)
    got_sums = lax.ppermute(sent, "core", SWAP)
    terms, acts = block_products(
        core, sums, got_sums, w_gate, w_up, w_down, other_cols, dp_count
    )
    summed = lax.psum_scatter(
        terms.reshape(dp_count * z_count * slots, 2 * width),
        PLANE,
        scatter_dimension=0,
        tiled=True,
    )
    *grads, away = weight_grads(core, acts, gathered)
    grads = fill_columns(core, grads, lax.ppermute(away, "core", SWAP))
    summed, grads = lax.optimization_barrier((summed, grads))
    summed = summed.reshape(expert_count, CAP, 2 * width)
    returned = lax.all_to_all(summed, "expert", split_axis=0, concat_axis=0, tiled=True)
    expert_out = returned[:, :, :width].astype(jnp.float32) * slot_gate[:, :, None]
    expert_back = returned[:, :, width:].astype(jnp.float32)
    mixed = jnp.einsum(
        "jct,jcf->tf", slot_table, expert_out, precision=lax.Precision.HIGHEST
    ).astype(jnp.bfloat16)
    grad_tokens = jnp.einsum(
        "jct,jcf->tf", slot_table, expert_back, precision=lax.Precision.HIGHEST
    ).astype(jnp.bfloat16)
    return (mixed, grad_tokens, *grads)


def solution(mesh):
    dp, expert, tensor = (mesh.shape[a] for a in ("dp", "expert", "tensor"))
    fine = Mesh(mesh.devices.reshape(dp, expert, tensor // 2, 2), ("dp", "expert", "z", "core"))
    feats = P(("dp", "expert"), ("z", "core"))
    ids = P(("dp", "expert"), None)
    weights = P("expert", ("dp", "z", "core"), None)
    return jax.shard_map(
        on_device,
        mesh=fine,
        in_specs=(feats, feats, ids, ids, weights, weights, weights),
        out_specs=(feats, feats, weights, weights, weights),
        check_vma=False,
    )
```

time: 247 us -> 254 us (1.028)
  Pallas kernels: 43.2 us -> 50.2 us
    ppermute x1 -> x2, waiting for transfers between devices: 2.02 us -> 13.4 us  [the longest x1 10.1 us: on_device(): grads = fill_columns(core, grads, lax.ppermute(away, 'core', SWAP))]
    reduce_scatter x1, waiting for transfers between devices: 73 us -> 62 us  [on_device(): lax.psum_scatter(terms.reshape(dp_count * z_count * slots, 2 * width), PL...]
    all_gather x1, waiting for transfers between devices: 72.6 us -> 64.9 us  [on_device(): gathered = lax.all_gather(shard, PLANE, axis=0, tiled=True)]
    pallas_call x3 -> x4, Pallas kernels: 40.9 us -> 47.9 us  [the longest x1 20.5 us: forward(): pl.pallas_call(kernel, out_shape=[jax.ShapeDtypeStruct((6, hidden, rows),...]
    ppermute x1, waiting for transfers between devices: 0.01 us -> 5.93 us  [on_device(): other_cols = lax.ppermute(packed, 'core', SWAP)]
    unnamed x10 -> x16, local copies, waits for them, and re-layouts: 4.75 us -> 7.26 us
  transfers between devices with their start and end apart: 5 -> 6, of which waited for: 4 -> 6; matrix products, arithmetic and copies ran while one was open for 0% -> 0% of each run, Pallas kernels for 13% -> 7%
where the time goes in v2:
time: 254 us
  waiting for transfers between devices  156 us (61%)
  Pallas kernels  50.2 us (20%)
  between operations  14.1 us (6%)
  blocking collectives  13 us (5%)
  local copies, waits for them, and re-layouts  7.47 us (3%)
  starting transfers between devices  4.61 us (2%)
  other arithmetic  4.01 us (2%)
  matrix products  3.8 us (1%)
    all_gather x1, waiting for transfers between devices, on_device(): gathered = lax.all_gather(shard, PLANE, axis=0, tiled=True)  64.9 us
    reduce_scatter x1, waiting for transfers between devices, on_device(): lax.psum_scatter(terms.reshape(dp_count * z_count * slots, 2 * width), PL...  62 us
    pallas_call x1, Pallas kernels, forward(): pl.pallas_call(kernel, out_shape=[jax.ShapeDtypeStruct((6, hidden, rows),...  20.5 us
    pallas_call x1, Pallas kernels, block_products(): pl.pallas_call(kernel, out_shape=[jax.ShapeDtypeStruct((dp, z_count, slot...  13.2 us
    all_to_all x1, blocking collectives, on_device(): lax.all_to_all(summed, 'expert', split_axis=0, concat_axis=0, tiled=True)  13 us
    pallas_call x1, Pallas kernels, weight_grads(): pl.pallas_call(kernel, out_shape=[out] * 3 + [jax.ShapeDtypeStruct((3, z_...  11 us
    all_to_all x1, waiting for transfers between devices, on_device(): lax.all_to_all(jnp.concatenate([send_rows, send_cots], axis=1), 'expert',...  10.2 us
    ppermute x1, waiting for transfers between devices, on_device(): grads = fill_columns(core, grads, lax.ppermute(away, 'core', SWAP))  10.1 us
  transfers between devices with their start and end apart: 6, of which 6 were waited for; matrix products, arithmetic and copies ran while one was open for 0% of the time, Pallas kernels for 7%

profile of v2, /device:TPU:0, one launch (start us, length us, event | category | flops | bytes accessed | tf_op | source)
XLA Modules:
  0.0 253.7 jit_solution(13149822416128162293)
XLA Ops:
  7.2 0.0 copy-start
  7.2 0.7 fusion.25
  7.9 0.7 convert_multiply_fusion
  8.6 0.7 select_reduce_fusion
  9.3 0.1 copy.25
  9.4 0.2 reduce_window_sum.11
  9.6 0.1 copy.26
  9.7 0.2 fusion.13
  9.9 0.0 copy-done
  9.9 0.0 copy-start.2
  9.9 0.2 convolution_convert_fusion
  10.1 1.3 fusion
  11.4 0.9 pad_maximum_fusion
  12.2 4.4 %all-to-all-start = ((bf16[4,96,768]{2,1,0:T(8,128)(2,1)}), bf16[4,96,768]{2,1,0:T(8,128)(2,1)S(1)}, u32[]{:S(2)}, u32[]{:S(2)}) async-start(bf16[4,96,768]{2,1,0:T(8,128)(2,1)} %pad_maximum_fusion), calls=%async_computation | async-start | bytes 1179648 | tf_op jit(solution)/shard_map/all_to_all | solution.py:268
  16.6 0.0 all-gather.2.cloned.1.call-start
  16.6 10.2 %all-to-all-done = bf16[4,96,768]{2,1,0:T(8,128)(2,1)S(1)} async-done(((bf16[4,96,768]{2,1,0:T(8,128)(2,1)}), bf16[4,96,768]{2,1,0:T(8,128)(2,1)S(1)}, u32[]{:S(2)}, u32[]{:S(2)}) %all-to-all-start) | async-done | bytes 589856 | tf_op jit(solution)/shard_map/all_to_all | solution.py:268
  26.9 0.9 pad_maximum_fusion.1
  27.7 0.0 all-gather.2.cloned.1.call-update
  27.7 0.0 reduce-scatter.2.cloned.1.call-start
  27.8 0.0 copy-done.2
  27.8 0.0 copy-start.3
  27.8 1.6 copy-done.3
  29.4 0.0 copy-start.5
  29.4 1.6 copy-done.5
  31.0 2.3 pack_columns.1
  33.3 0.0 collective-permute-start
  33.3 5.9 %collective-permute-done.oc_ref = bf16[3,4,168,768]{3,2,1,0:T(8,128)(2,1)} collective-permute-done((bf16[3,4,168,768]{3,2,1,0:T(8,128)(2,1)}, bf16[3,4,168,768]{3,2,1,0:T(8,128)(2,1)}, u32[]{:S(2)}, u32[]{:S(2)}) %collective-permute-start) | collective-permute-done | bytes 3096608 | tf_op jit(solution)/shard_map/ppermute | solution.py:283
  39.2 64.9 %all-gather.2.cloned.1.call-done = bf16[6144,768]{1,0:T(8,128)(2,1)} async-done(((bf16[384,768]{1,0:T(8,128)(2,1)}), bf16[6144,768]{1,0:T(8,128)(2,1)}) %all-gather.2.cloned.1.call-update) | async-done | bytes 9437200 | tf_op jit(solution)/shard_map/all_gather | solution.py:280
  104.1 0.0 copy-start.4
  104.1 1.6 copy-done.4
  105.7 20.5 %forward.1 = (f32[6,168,768]{2,1,0:T(8,128)}, bf16[6,168,768]{2,1,0:T(8,128)(2,1)S(1)}) custom-call(s32[1]{0:T(128)} %bitcast.2.core_ref, bf16[4,4,2,192,768]{4,3,2,1,0:T(8,128)(2,1)} %bitcast.30, bf16[1,168,6144]{2,1,0:T(8,128)(2,1)S(1)} %copy-done.2, bf16[1,168,6144]{2,1,0:T(8,128)(2,1)S(1)} %copy-done.4, bf16[1,168,6144]{2,1,0:T(8,128)(2,1)} %d_ref.5, ...), custom_call_target="tpu_custom_call" | custom-call | flops 4756340736 | bytes 15630336 | tf_op jit(solution)/shard_map/forward/pallas_call | solution.py:91
  126.1 0.0 collective-permute-start.1
  126.1 3.4 %collective-permute-done.1.r_ref = bf16[6,168,768]{2,1,0:T(8,128)(2,1)S(1)} collective-permute-done((bf16[6,168,768]{2,1,0:T(8,128)(2,1)S(1)}, bf16[6,168,768]{2,1,0:T(8,128)(2,1)S(1)}, u32[]{:S(2)}, u32[]{:S(2)}) %collective-permute-start.1) | collective-permute-done | bytes 1548320 | tf_op jit(solution)/shard_map/ppermute | solution.py:285
  129.5 13.2 %block_products.1 = (bf16[4,4,192,1536]{3,2,1,0:T(8,128)(2,1)}, bf16[6,168,768]{2,1,0:T(8,128)(2,1)S(1)}) custom-call(s32[1]{0:T(128)} %bitcast.2.core_ref, f32[6,168,768]{2,1,0:T(8,128)} %get-tuple-element.24.s_ref, bf16[6,168,768]{2,1,0:T(8,128)(2,1)S(1)} %collective-permute-done.1.r_ref, bf16[1,168,6144]{2,1,0:T(8,128)(2,1)S(1)} %copy-done.2, ...), custom_call_target="tpu_custom_call" | custom-call | flops 4756340736 | bytes 15630336 | tf_op jit(solution)/shard_map/block_products/pallas_call | solution.py:154
  142.7 0.0 copy-start.6
  142.7 1.1 copy-done.6
  143.8 0.0 copy-start.7
  143.8 0.0 reduce-scatter.2.cloned.1.call-update
  143.9 1.4 copy-done.7
  145.2 11.0 %weight_grads.1 = (f32[1,168,6144]{2,1,0:T(8,128)}, f32[1,168,6144]{2,1,0:T(8,128)}, f32[1,168,6144]{2,1,0:T(8,128)}, f32[3,4,168,768]{3,2,1,0:T(8,128)}) custom-call(s32[1]{0:T(128)} %bitcast.2.core_ref, bf16[6,168,768]{2,1,0:T(8,128)(2,1)S(1)} %copy-done.7, bf16[4,4,2,192,768]{4,3,2,1,0:T(8,128)(2,1)} %bitcast.31), custom_call_target="tpu_custom_call" | custom-call | flops 4756340736 | bytes 21823488 | tf_op jit(solution)/shard_map/weight_grads/pallas_call | solution.py:204
  156.2 0.2 collective-permute-start.2
  156.4 10.1 %collective-permute-done.2.got_ref = f32[3,4,168,768]{3,2,1,0:T(8,128)S(1)} collective-permute-done((f32[3,4,168,768]{3,2,1,0:T(8,128)}, f32[3,4,168,768]{3,2,1,0:T(8,128)S(1)}, u32[]{:S(2)}, u32[]{:S(2)}) %collective-permute-start.2) | collective-permute-done | bytes 6193184 | tf_op jit(solution)/shard_map/ppermute | solution.py:296
  166.4 0.0 copy-start.1
  166.4 3.3 %fill_columns.1 = (f32[1,168,6144]{2,1,0:T(8,128)}, f32[1,168,6144]{2,1,0:T(8,128)}, f32[1,168,6144]{2,1,0:T(8,128)}) custom-call(s32[1]{0:T(128)} %bitcast.2.core_ref, f32[3,4,168,768]{3,2,1,0:T(8,128)S(1)} %collective-permute-done.2.got_ref, f32[1,168,6144]{2,1,0:T(8,128)} %get-tuple-element.29.g_in, ...), custom_call_target="tpu_custom_call", output_to_operand_aliasing={{0}: (2, {}), {1}: (3, {}), {2}: (4, {})} | custom-call | bytes 12386304 | tf_op jit(solution)/shard_map/fill_columns/pallas_call | solution.py:236
  169.7 62.0 %reduce-scatter.2.cloned.1.call-done = bf16[192,1536]{1,0:T(8,128)(2,1)} async-done(((bf16[3072,1536]{1,0:T(8,128)(2,1)}), bf16[192,1536]{1,0:T(8,128)(2,1)}) %reduce-scatter.2.cloned.1.call-update) | async-done | bytes 589840 | tf_op jit(solution)/shard_map/reduce_scatter | solution.py:289
  231.7 13.0 %all_to_all.10 = bf16[4,48,1536]{2,1,0:T(8,128)(2,1)S(1)} all-to-all(bf16[4,48,1536]{2,1,0:T(8,128)(2,1)} %bitcast.35), channel_id=1, replica_groups=mesh['dp'=4,'expert'=4,'z'=4,'core'=2] {'expert'}, dimensions={0} | all-to-all | bytes 1179648 | tf_op jit(solution)/shard_map/all_to_all | solution.py:299
  244.7 1.2 fusion.1
  245.9 0.9 fusion.2
  246.8 0.0 copy-done.1
  (3 shorter events, 0.1 us)
Async XLA Ops:
  7.2 2.7 %copy-start = (bf16[128,768]{1,0:T(8,128)(2,1)S(1)}, bf16[128,768]{1,0:T(8,128)(2,1)}, u32[]{:S(2)}) copy-start(bf16[128,768]{1,0:T(8,128)(2,1)} %param.7) | copy-start | bytes 589828
  9.9 17.9 %copy-start.2 = (bf16[1,168,6144]{2,1,0:T(8,128)(2,1)S(1)}, bf16[1,168,6144]{2,1,0:T(8,128)(2,1)}, u32[]{:S(2)}) copy-start(bf16[1,168,6144]{2,1,0:T(8,128)(2,1)} %g_ref.5) | copy-start | bytes 6193156
  12.2 14.6 %all-to-all-start = ((bf16[4,96,768]{2,1,0:T(8,128)(2,1)}), bf16[4,96,768]{2,1,0:T(8,128)(2,1)S(1)}, u32[]{:S(2)}, u32[]{:S(2)}) async-start(bf16[4,96,768]{2,1,0:T(8,128)(2,1)} %pad_maximum_fusion), calls=%async_computation | async-start | bytes 1179648 | tf_op jit(solution)/shard_map/all_to_all | solution.py:268
  16.6 87.5 %all-gather.2.cloned.1.call-start = ((), (), s32[]{:S(2)}) async-start(), calls=%async_computation.3 | async-start | bytes 10027008 | tf_op jit(solution)/shard_map/all_gather | solution.py:280
  27.7 203.9 %reduce-scatter.2.cloned.1.call-start = ((), (), s32[]{:S(2)}) async-start(), calls=%async_computation.4 | async-start | bytes 10027008 | tf_op jit(solution)/shard_map/reduce_scatter | solution.py:289
  27.8 1.6 copy-start.3
  29.4 1.6 copy-start.5
  33.3 5.9 %collective-permute-start = (bf16[3,4,168,768]{3,2,1,0:T(8,128)(2,1)}, bf16[3,4,168,768]{3,2,1,0:T(8,128)(2,1)}, u32[]{:S(2)}, u32[]{:S(2)}) collective-permute-start(bf16[3,4,168,768]{3,2,1,0:T(8,128)(2,1)} %pack_columns.1), channel_id=1, source_target_pairs={{0,1},{1,0},{2,3},{3,2},{4,5},{5,4},{6,7},{7,6},{8,9},{9,8},{10,11... | collective-permute-start | bytes 9289736 | tf_op jit(solution)/shard_map/ppermute | solution.py:283
  104.1 1.6 copy-start.4
  126.1 3.4 %collective-permute-start.1 = (bf16[6,168,768]{2,1,0:T(8,128)(2,1)S(1)}, bf16[6,168,768]{2,1,0:T(8,128)(2,1)S(1)}, u32[]{:S(2)}, u32[]{:S(2)}) collective-permute-start(bf16[6,168,768]{2,1,0:T(8,128)(2,1)S(1)} %get-tuple-element.25), channel_id=1, source_target_pairs={{0,1},{1,0},{2,3},{3,2},{4,5},{5,4},{6,7},{7,6},{8,9},{9,8},{10,11... | collective-permute-start | bytes 4644872 | tf_op jit(solution)/shard_map/ppermute | solution.py:285
  142.7 1.1 copy-start.6
  143.8 1.4 copy-start.7
  156.2 10.2 %collective-permute-start.2 = (f32[3,4,168,768]{3,2,1,0:T(8,128)}, f32[3,4,168,768]{3,2,1,0:T(8,128)S(1)}, u32[]{:S(2)}, u32[]{:S(2)}) collective-permute-start(f32[3,4,168,768]{3,2,1,0:T(8,128)} %get-tuple-element.28), channel_id=1, source_target_pairs={{0,1},{1,0},{2,3},{3,2},{4,5},{5,4},{6,7},{7,6},{8,9},{9,8},{10,11... | collective-permute-start | bytes 18579464 | tf_op jit(solution)/shard_map/ppermute | solution.py:296
  166.4 80.4 %copy-start.1 = (bf16[128,768]{1,0:T(8,128)(2,1)S(1)}, bf16[128,768]{1,0:T(8,128)(2,1)}, u32[]{:S(2)}) copy-start(bf16[128,768]{1,0:T(8,128)(2,1)} %param.7) | copy-start | bytes 589828
Sparse Core Ops, SparseCore 0:
  27.9 76.2 all-gather.1
  144.0 87.6 reduce-scatter.1
